TPU v7x, 32 devices: a whole 2x2x4 slice. The times are simulated.
32 devices in a mesh: dp: 16 (over z, x, core), tensor: 2 (over y).
Axes of the slice: x: 2, y: 2, z: 4, core: 2. Of those that a mesh axis runs over, the one named last changes fastest.
Arguments:
- hidden_in: bfloat16 [4096, 1536], P(('dp', 'tensor')), may hold values from -6 to 6
- cotangent: float32 [4096, 1536], P(('dp', 'tensor')), may hold values from -6 to 6
- segments: int32 [16, 256], P('dp'), may hold values from 0 to 3, as said below
- positions: int32 [16, 256], P('dp'), may hold values from 0 to 127, as said below
- norm_gains: bfloat16 [1, 2, 1536], P(None, None, 'dp'), may hold values from 0.099609375 to 1.8984375
- q_weight: bfloat16 [1, 1536, 1536], P(None, 'dp', 'tensor'), may hold values from -0.15625 to 0.15625
- k_weight: bfloat16 [1, 1536, 256], P(None, 'dp', 'tensor'), may hold values from -0.15625 to 0.15625
- v_weight: bfloat16 [1, 1536, 256], P(None, 'dp', 'tensor'), may hold values from -0.15625 to 0.15625
- q_bias: bfloat16 [1, 12, 128], P(None, 'tensor', 'dp'), may hold values from -3 to 3
- k_bias: bfloat16 [1, 2, 128], P(None, 'tensor', 'dp'), may hold values from -3 to 3
- v_bias: bfloat16 [1, 2, 128], P(None, 'tensor', 'dp'), may hold values from -3 to 3
- o_weight: bfloat16 [1, 1536, 1536], P(None, 'tensor', 'dp'), may hold values from -0.625 to 0.625
- gate_weight: bfloat16 [1, 1536, 8960], P(None, 'dp', 'tensor'), may hold values from -0.15625 to 0.15625
- up_weight: bfloat16 [1, 1536, 8960], P(None, 'dp', 'tensor'), may hold values from -0.15625 to 0.15625
- down_weight: bfloat16 [1, 8960, 1536], P(None, 'tensor', 'dp'), may hold values from -0.0625 to 0.0625
Outputs:
- hidden_out: float32 [4096, 1536], P(('dp', 'tensor'))
- input_grad: float32 [4096, 1536], P(('dp', 'tensor'))
- gain_grads: float32 [1, 2, 1536], P(None, None, ('dp', 'tensor'))
- q_weight_grad: float32 [1, 1536, 1536], P(None, 'dp', 'tensor')
- k_weight_grad: float32 [1, 1536, 256], P(None, 'dp', 'tensor')
- v_weight_grad: float32 [1, 1536, 256], P(None, 'dp', 'tensor')
- o_weight_grad: float32 [1, 1536, 1536], P(None, 'tensor', 'dp')
- q_bias_grad: float32 [1, 12, 128], P(None, 'tensor', 'dp')
- k_bias_grad: float32 [1, 2, 128], P(None, 'tensor')
- v_bias_grad: float32 [1, 2, 128], P(None, 'tensor', 'dp')
- gate_weight_grad: float32 [1, 1536, 8960], P(None, 'dp', 'tensor')
- up_weight_grad: float32 [1, 1536, 8960], P(None, 'dp', 'tensor')
- down_weight_grad: float32 [1, 8960, 1536], P(None, 'tensor', 'dp')
Inputs may be any that keep to these rules, and one draw needn't show every extreme that they name: `segments`: document numbers never fall along a sequence and rise by one where a document starts; every sequence holds exactly 4 documents, one of them 256 / 2 tokens long. `positions`: A token's position within its document, 0 at the document's first token and rising by one.
All inputs are finite; a program needn't handle non-finite values.
Results may differ from a plain program's by a relative error of at most 0.02.
Values may be sent and summed in bfloat16 or wider, within the bound.
No kernel may reach another device: no remote copies, remote signals or barrier semaphores. Data moves between devices by JAX's collectives and lax.ppermute only.
A program may use at most 256 MiB of HBM per device.

v0:
```python
import jax
import jax.numpy as jnp
from jax import lax
from jax.sharding import PartitionSpec as P

HD = 128
LAYERS = 1
eps = 1e-06
theta_log = 13.815510557964274


def product(form, left, right):
    return jnp.einsum(form, left, right, preferred_element_type=jnp.float32)


def rope_tables(position_ids, head_width):
    half_width = head_width // 2
    freq_index = jnp.arange(half_width).astype(jnp.float32)
    frequency = jnp.exp(-(2.0 * freq_index / head_width) * theta_log)
    angles = position_ids.astype(jnp.float32)[..., None] * frequency
    return (jnp.cos(angles), jnp.sin(angles))


def rotate(vectors, cosine, sine_table):
    half_width = vectors.shape[-1] // 2
    first_half = vectors[..., :half_width]
    second_half = vectors[..., half_width:]
    cos_wide = cosine[:, :, None, :]
    sin_wide = sine_table[:, :, None, :]
    return jnp.concatenate(
        [
            first_half * cos_wide - second_half * sin_wide,
            second_half * cos_wide + first_half * sin_wide,
        ],
        axis=-1,
    )


def unrotate(vectors, cosine, sine_table):
    half_width = vectors.shape[-1] // 2
    first_half = vectors[..., :half_width]
    second_half = vectors[..., half_width:]
    cos_wide = cosine[:, :, None, :]
    sin_wide = sine_table[:, :, None, :]
    return jnp.concatenate(
        [
            first_half * cos_wide + second_half * sin_wide,
            second_half * cos_wide - first_half * sin_wide,
        ],
        axis=-1,
    )


def norm_forward(stream, gain_vec):
    inv_scale = lax.rsqrt(jnp.mean(stream * stream, axis=-1, keepdims=True) + eps)
    unit_rows = stream * inv_scale
    return ((unit_rows * gain_vec.astype(jnp.float32)).astype(jnp.bfloat16), unit_rows, inv_scale)


def norm_backward(d_normed, unit_rows, inv_scale, gain_vec):
    d_unit = d_normed * gain_vec.astype(jnp.float32)
    d_gain = jnp.sum(d_normed * unit_rows, axis=0)
    d_stream = inv_scale * (
        d_unit - unit_rows * jnp.mean(d_unit * unit_rows, axis=-1, keepdims=True)
    )
    return (d_stream, d_gain)


def attend(queries, key_vecs, value_vecs, allowed, scale):
    scores = product("bqngd,bknd->bngqk", queries, key_vecs) * scale
    expo = jnp.exp(scores) * allowed[:, None, None]
    denom_sum = jnp.sum(expo, axis=-1, keepdims=True)
    attention = (expo / denom_sum).astype(jnp.bfloat16)
    mixed = product("bngqk,bknd->bqngd", attention, value_vecs).astype(jnp.bfloat16)
    return (mixed, jnp.log(denom_sum))


def attend_backward(queries, key_vecs, value_vecs, allowed, log_total, d_mixed, scale):
    scores = product("bqngd,bknd->bngqk", queries, key_vecs) * scale
    probs_f = jnp.exp(scores - log_total) * allowed[:, None, None]
    d_value = product("bngqk,bqngd->bknd", probs_f.astype(jnp.bfloat16), d_mixed)
    d_probs = product("bqngd,bknd->bngqk", d_mixed, value_vecs)
    centre = jnp.sum(probs_f * d_probs, axis=-1, keepdims=True)
    d_scores = (probs_f * (d_probs - centre) * scale).astype(jnp.bfloat16)
    d_query = product("bngqk,bknd->bqngd", d_scores, key_vecs)
    d_key = product("bngqk,bqngd->bknd", d_scores, queries)
    return (d_query, d_key, d_value)


def attn_forward(rows_in, weights, cosine, sine_table, allowed, sequences):
    w_query, w_key, w_value, w_out, b_query, b_key, b_value = weights[:7]
    head_count, head_width = b_query.shape
    group_count = b_key.shape[0]
    group_size = head_count // group_count
    row_count = rows_in.shape[0]
    span_length = row_count // sequences
    queries = jnp.dot(rows_in, w_query, preferred_element_type=jnp.float32) + b_query.reshape(
        -1
    ).astype(jnp.float32)
    key_vecs = jnp.dot(rows_in, w_key, preferred_element_type=jnp.float32) + b_key.reshape(
        -1
    ).astype(jnp.float32)
    value_vecs = (
        jnp.dot(rows_in, w_value, preferred_element_type=jnp.float32)
        + b_value.reshape(-1).astype(jnp.float32)
    ).astype(jnp.bfloat16)
    queries = rotate(
        queries.reshape(sequences, span_length, head_count, head_width), cosine, sine_table
    ).astype(jnp.bfloat16)
    queries = queries.reshape(sequences, span_length, group_count, group_size, head_width)
    key_vecs = rotate(
        key_vecs.reshape(sequences, span_length, group_count, head_width), cosine, sine_table
    ).astype(jnp.bfloat16)
    value_vecs = value_vecs.reshape(sequences, span_length, group_count, head_width)
    mixed, log_total = attend(queries, key_vecs, value_vecs, allowed, head_width ** (-0.5))
    attn_rows = mixed.reshape(row_count, head_count * head_width)
    branch = jnp.dot(attn_rows, w_out, preferred_element_type=jnp.float32)
    return (branch, (queries, key_vecs, value_vecs, log_total, attn_rows))


def attn_backward(rows_in, weights, stored, d_out, cosine, sine_table, allowed, sequences):
    w_query, w_key, w_value, w_out, b_query, b_key, b_value = weights[:7]
    head_count, head_width = b_query.shape
    group_count = b_key.shape[0]
    queries, key_vecs, value_vecs, log_total, attn_rows = stored
    row_count = rows_in.shape[0]
    span_length = row_count // sequences
    d_o_weight = jnp.dot(attn_rows.T, d_out, preferred_element_type=jnp.float32)
    d_mixed = (
        jnp.dot(d_out, w_out.T, preferred_element_type=jnp.float32)
        .astype(jnp.bfloat16)
        .reshape(queries.shape)
    )
    d_query, d_key, d_value = attend_backward(
        queries, key_vecs, value_vecs, allowed, log_total, d_mixed, head_width ** (-0.5)
    )
    d_query = unrotate(
        d_query.reshape(sequences, span_length, head_count, head_width), cosine, sine_table
    ).reshape(row_count, -1)
    d_key = unrotate(d_key, cosine, sine_table).reshape(row_count, -1)
    d_value = d_value.reshape(row_count, -1)
    d_b_query = jnp.sum(d_query, axis=0).reshape(head_count, head_width)
    d_b_key = jnp.sum(d_key, axis=0).reshape(group_count, head_width)
    d_b_value = jnp.sum(d_value, axis=0).reshape(group_count, head_width)
    query_low = d_query.astype(jnp.bfloat16)
    key_low = d_key.astype(jnp.bfloat16)
    value_low = d_value.astype(jnp.bfloat16)
    d_rows = jnp.dot(query_low, w_query.T, preferred_element_type=jnp.float32)
    d_rows = d_rows + jnp.dot(key_low, w_key.T, preferred_element_type=jnp.float32)
    d_rows = d_rows + jnp.dot(value_low, w_value.T, preferred_element_type=jnp.float32)
    grads = (
        jnp.dot(rows_in.T, query_low, preferred_element_type=jnp.float32),
        jnp.dot(rows_in.T, key_low, preferred_element_type=jnp.float32),
        jnp.dot(rows_in.T, value_low, preferred_element_type=jnp.float32),
        d_o_weight,
        d_b_query,
        d_b_key,
        d_b_value,
    )
    return (d_rows, grads)


def mlp_forward(rows_in, weights):
    w_gate, w_up, w_down = weights[:3]
    gate_pre = jnp.dot(rows_in, w_gate, preferred_element_type=jnp.float32)
    up_pre = jnp.dot(rows_in, w_up, preferred_element_type=jnp.float32)
    hidden_act = (jax.nn.silu(gate_pre) * up_pre).astype(jnp.bfloat16)
    return (
        jnp.dot(hidden_act, w_down, preferred_element_type=jnp.float32),
        (gate_pre, up_pre, hidden_act),
    )


def mlp_backward(rows_in, weights, stored, d_out):
    w_gate, w_up, w_down = weights[:3]
    gate_pre, up_pre, hidden_act = stored
    d_down = jnp.dot(hidden_act.T, d_out, preferred_element_type=jnp.float32)
    d_hidden = jnp.dot(d_out, w_down.T, preferred_element_type=jnp.float32)
    sigmoid_g = jax.nn.sigmoid(gate_pre)
    d_gate = (d_hidden * up_pre * sigmoid_g * (1.0 + gate_pre * (1.0 - sigmoid_g))).astype(
        jnp.bfloat16
    )
    d_up = (d_hidden * gate_pre * sigmoid_g).astype(jnp.bfloat16)
    d_rows = jnp.dot(d_gate, w_gate.T, preferred_element_type=jnp.float32) + jnp.dot(
        d_up, w_up.T, preferred_element_type=jnp.float32
    )
    grads = (
        jnp.dot(rows_in.T, d_gate, preferred_element_type=jnp.float32),
        jnp.dot(rows_in.T, d_up, preferred_element_type=jnp.float32),
        d_down,
    )
    return (d_rows, grads)


def per_device(
    hidden_in,
    cotangent,
    segments,
    positions,
    norm_gains,
    q_weight,
    k_weight,
    v_weight,
    q_bias,
    k_bias,
    v_bias,
    o_weight,
    gate_weight,
    up_weight,
    down_weight,
):
    sequences = segments.shape[0]
    span_length = segments.shape[1]
    cosine, sine_table = rope_tables(positions, HD)
    places = jnp.arange(span_length)
    causal = places[None, :] <= places[:, None]
    allowed = ((segments[:, :, None] == segments[:, None, :]) & causal[None]).astype(jnp.float32)

    def fetch_attn(layer_no):
        return (
            lax.all_gather(q_weight[layer_no], "dp", axis=0, tiled=True),
            lax.all_gather(k_weight[layer_no], "dp", axis=0, tiled=True),
            lax.all_gather(v_weight[layer_no], "dp", axis=0, tiled=True),
            lax.all_gather(o_weight[layer_no], "dp", axis=1, tiled=True),
            lax.all_gather(q_bias[layer_no], "dp", axis=1, tiled=True),
            lax.all_gather(k_bias[layer_no], "dp", axis=1, tiled=True),
            lax.all_gather(v_bias[layer_no], "dp", axis=1, tiled=True),
            lax.all_gather(norm_gains[layer_no, 0], "dp", axis=0, tiled=True),
        )

    def fetch_mlp(layer_no):
        return (
            lax.all_gather(gate_weight[layer_no], "dp", axis=0, tiled=True),
            lax.all_gather(up_weight[layer_no], "dp", axis=0, tiled=True),
            lax.all_gather(down_weight[layer_no], "dp", axis=1, tiled=True),
            lax.all_gather(norm_gains[layer_no, 1], "dp", axis=0, tiled=True),
        )

    def gather_rows(values_in):
        return lax.all_gather(values_in, "tensor", axis=0, tiled=True)

    def sum_rows(partial_value):
        return lax.psum_scatter(
            partial_value.astype(jnp.bfloat16), "tensor", scatter_dimension=0, tiled=True
        ).astype(jnp.float32)

    stream = hidden_in.astype(jnp.float32)
    layer_no = 0
    attn_w = fetch_attn(layer_no)
    normed_one, unit_one, inv_one = norm_forward(stream, attn_w[7])
    rows_one = gather_rows(normed_one)
    partial_value, stored_one = attn_forward(
        rows_one, attn_w, cosine, sine_table, allowed, sequences
    )
    mid_stream = stream + sum_rows(partial_value)
    mlp_w = fetch_mlp(layer_no)
    normed_two, unit_two, inv_two = norm_forward(mid_stream, mlp_w[3])
    rows_two = gather_rows(normed_two)
    partial_value, stored_two = mlp_forward(rows_two, mlp_w)
    stream = mid_stream + sum_rows(partial_value)
    held = None
    kept = [
        (rows_one, unit_one, inv_one, stored_one, rows_two, unit_two, inv_two, stored_two, held)
    ]
    gradient = cotangent
    attn_list = []
    mlp_list = []
    gain_list = []
    key_list = []
    for layer_no in reversed(range(LAYERS)):
        rows_one, unit_one, inv_one, stored_one, rows_two, unit_two, inv_two, stored_two, held = (
            kept[layer_no]
        )
        mlp_w = fetch_mlp(layer_no)
        attn_w = fetch_attn(layer_no)
        d_rows, mlp_grads = mlp_backward(
            rows_two, mlp_w, stored_two, gather_rows(gradient.astype(jnp.bfloat16))
        )
        d_norm, gain_two = norm_backward(sum_rows(d_rows), unit_two, inv_two, mlp_w[3])
        grad_mid = gradient + d_norm
        mlp_list.insert(
            0,
            (
                lax.psum_scatter(mlp_grads[0], "dp", scatter_dimension=0, tiled=True),
                lax.psum_scatter(mlp_grads[1], "dp", scatter_dimension=0, tiled=True),
                lax.psum_scatter(mlp_grads[2], "dp", scatter_dimension=1, tiled=True),
            ),
        )
        d_rows, attn_grads = attn_backward(
            rows_one,
            attn_w,
            stored_one,
            gather_rows(grad_mid.astype(jnp.bfloat16)),
            cosine,
            sine_table,
            allowed,
            sequences,
        )
        d_norm, gain_one = norm_backward(sum_rows(d_rows), unit_one, inv_one, attn_w[7])
        gradient = grad_mid + d_norm
        spread_grads = (
            attn_grads[0],
            attn_grads[1],
            attn_grads[2],
            attn_grads[3],
            attn_grads[4],
            attn_grads[6],
        )
        attn_list.insert(
            0,
            (
                lax.psum_scatter(spread_grads[0], "dp", scatter_dimension=0, tiled=True),
                lax.psum_scatter(spread_grads[1], "dp", scatter_dimension=0, tiled=True),
                lax.psum_scatter(spread_grads[2], "dp", scatter_dimension=0, tiled=True),
                lax.psum_scatter(spread_grads[3], "dp", scatter_dimension=1, tiled=True),
                lax.psum_scatter(spread_grads[4], "dp", scatter_dimension=1, tiled=True),
                lax.psum_scatter(spread_grads[5], "dp", scatter_dimension=1, tiled=True),
            ),
        )
        key_list.insert(0, attn_grads[5])
        gain_list.insert(0, jnp.stack([gain_one, gain_two]))
    gain_grads = lax.psum_scatter(
        jnp.stack(gain_list), ("dp", "tensor"), scatter_dimension=2, tiled=True
    )
    key_bias_grad = lax.psum(jnp.stack(key_list), "dp")
    attn_out = tuple((jnp.stack([entry[index] for entry in attn_list]) for index in range(6)))
    mlp_out = tuple((jnp.stack([entry[index] for entry in mlp_list]) for index in range(3)))
    return (
        stream,
        gradient,
        gain_grads,
        attn_out[0],
        attn_out[1],
        attn_out[2],
        attn_out[3],
        attn_out[4],
        key_bias_grad,
        attn_out[5],
        mlp_out[0],
        mlp_out[1],
        mlp_out[2],
    )


def solution(mesh):
    return jax.shard_map(
        per_device,
        mesh=mesh,
        in_specs=(
            P(("dp", "tensor"), None),
            P(("dp", "tensor"), None),
            P("dp", None),
            P("dp", None),
            P(None, None, "dp"),
            P(None, "dp", "tensor"),
            P(None, "dp", "tensor"),
            P(None, "dp", "tensor"),
            P(None, "tensor", "dp"),
            P(None, "tensor", "dp"),
            P(None, "tensor", "dp"),
            P(None, "tensor", "dp"),
            P(None, "dp", "tensor"),
            P(None, "dp", "tensor"),
            P(None, "tensor", "dp"),
        ),
        out_specs=(
            P(("dp", "tensor"), None),
            P(("dp", "tensor"), None),
            P(None, None, ("dp", "tensor")),
            P(None, "dp", "tensor"),
            P(None, "dp", "tensor"),
            P(None, "dp", "tensor"),
            P(None, "tensor", "dp"),
            P(None, "tensor", "dp"),
            P(None, "tensor", None),
            P(None, "tensor", "dp"),
            P(None, "dp", "tensor"),
            P(None, "dp", "tensor"),
            P(None, "tensor", "dp"),
        ),
        check_vma=False,
    )
```

profile of v0, /device:TPU:0, one launch (start us, length us, event | category | flops | bytes accessed | tf_op | source)
XLA Modules:
  0.0 1799.2 jit_solution(1641613084074922660)
XLA Ops:
  8.7 1.3 fusion.116
  15.7 37.0 %all-reduce.7 = (bf16[1536]{0:T(1024)(128)(2,1)S(1)}, bf16[128]{0:T(256)(128)(2,1)S(1)}, bf16[128]{0:T(256)(128)(2,1)S(1)}, bf16[1536]{0:T(1024)(128)(2,1)}) all-reduce(bf16[1536]{0:T(1024)(128)(2,1)S(1)} %dynamic-update-slice, bf16[128]{0:T(256)(128)(2,1)S(1)} %dynamic-update-slice.1, ...), channel_id=2, replica_groups=mesh['dp'=16,'tensor'=2] {'dp'}, use_global_device_ids=true, to_apply=%add | all-reduce | flops 3328 | bytes 13312
  52.7 17.3 all-gather.6
  70.0 1.2 fusion.65
  71.2 21.7 %all-gather.1 = bf16[1,1536,128]{2,1,0:T(8,128)(2,1)S(1)} all-gather(bf16[1,96,128]{2,1,0:T(8,128)(2,1)} %param.22), channel_id=3, replica_groups=mesh['dp'=16,'tensor'=2] {'dp'}, dimensions={1}, use_global_device_ids=true | all-gather | bytes 417792 | tf_op jit(solution)/shard_map/all_gather | solution.py:223
  93.5 1.2 fusion.62
  94.7 12.0 all_gather.58
  107.7 18.2 %all-gather.3 = bf16[1,1536,128]{2,1,0:T(8,128)(2,1)S(1)} all-gather(bf16[1,96,128]{2,1,0:T(8,128)(2,1)S(1)} %copy-done.33), channel_id=5, replica_groups=mesh['dp'=16,'tensor'=2] {'dp'}, dimensions={1}, use_global_device_ids=true | all-gather | bytes 417792 | tf_op jit(solution)/shard_map/all_gather | solution.py:222
  127.3 1.2 multiply_cosine_fusion
  128.7 2.4 fusion.36
  132.0 1.2 fusion.71
  135.2 3.5 convolution_convert_fusion
  141.2 1.2 convert_element_type.173
  142.4 20.3 %all_gather.71 = bf16[256,1536]{1,0:T(8,128)(2,1)} all-gather(bf16[128,1536]{1,0:T(8,128)(2,1)S(1)} %convert_element_type.173), channel_id=1, replica_groups=mesh['dp'=16,'tensor'=2] {'tensor'}, dimensions={0}, use_global_device_ids=true | all-gather | bytes 1179648 | tf_op jit(solution)/shard_map/all_gather | solution.py:240
  163.6 1.2 multiply_reduce_fusion
  165.4 1.2 multiply_convert_fusion.3
  166.6 11.7 all_gather.67
  178.2 94.6 %all-gather.24.cloned.1.call-done = bf16[1,1536,4480]{2,1,0:T(8,128)(2,1)} async-done(((bf16[1,96,4480]{2,1,0:T(8,128)(2,1)}), bf16[1,1536,4480]{2,1,0:T(8,128)(2,1)}) %all-gather.24.cloned.1.call-update) | async-done | bytes 13762576 | tf_op jit(solution)/shard_map/all_gather | solution.py:234
  272.8 11.1 fusion.6
  283.9 96.9 %all-gather.26.cloned.1.call-done = bf16[1,4480,1536]{1,2,0:T(8,128)(2,1)} async-done(((bf16[1,4480,96]{1,2,0:T(8,128)(2,1)}), bf16[1,4480,1536]{1,2,0:T(8,128)(2,1)}) %all-gather.26.cloned.1.call-update) | async-done | bytes 13762576 | tf_op jit(solution)/shard_map/all_gather | solution.py:235
  380.9 11.0 fusion
  391.9 97.0 %all-gather.22.cloned.1.call-done = bf16[1,1536,4480]{2,1,0:T(8,128)(2,1)} async-done(((bf16[1,96,4480]{2,1,0:T(8,128)(2,1)}), bf16[1,1536,4480]{2,1,0:T(8,128)(2,1)}) %all-gather.22.cloned.1.call-update) | async-done | bytes 13762576 | tf_op jit(solution)/shard_map/all_gather | solution.py:233
  488.9 14.5 multiply_convert_fusion.1
  503.4 8.7 fusion.4
  512.1 8.3 fusion.18
  520.4 1.3 log.8
  521.7 14.5 reduce-scatter.21.cloned.1.call-done
  536.2 2.1 fusion.59
  538.9 1.6 fusion.114
  540.5 11.3 all_gather.72
  552.7 1.5 fusion.40
  554.3 1.9 copy.80
  556.2 2.6 fusion.117
  563.7 1.2 copy.84
  564.9 2.5 fusion.25
  568.5 1.3 fusion.21
  569.8 10.3 fusion.15
  580.2 1.3 stack.40
  581.5 5.9 reduce-scatter.23.cloned.1.call-done
  587.4 1.9 fusion.64
  589.3 1.3 maximum_bitcast_fusion.3
  590.6 2.4 copy.100
  593.3 2.2 fusion.98
  595.5 2.3 fusion.105
  597.9 2.9 fusion.118
  600.9 1.1 copy-done.15
  602.1 2.9 fusion.119
  605.1 1.1 copy-done.3
  606.1 12.8 fusion.120
  619.0 12.9 fusion.121
  632.0 1.1 copy-done.16
  633.1 13.0 fusion.122
  646.8 1.5 fusion.81
  649.2 34.1 %all-reduce.6 = (f32[6,128]{1,0:T(8,128)S(1)}, f32[1,1,128]{2,1,0:T(1,128)}, f32[1,128]{1,0:T(1,128)S(1)}) all-reduce(f32[6,128]{1,0:T(8,128)} %fusion.79, f32[1,1,128]{2,1,0:T(1,128)} %bitcast.241, f32[1,128]{1,0:T(1,128)} %bitcast.240), channel_id=23, replica_groups=mesh['dp'=16,'tensor'=2] {'dp'}, use_global_device_ids=true, to_apply=%region_18.19.clone | all-reduce | flops 1024 | bytes 8192
  685.2 2.8 fusion.55
  688.0 21.0 %reduce-scatter.39.cloned.1.call-done = f32[48,2]{1,0:T(8,128)} async-done(((f32[1536,2]{1,0:T(8,128)}), f32[48,2]{1,0:T(8,128)}) %reduce-scatter.39.cloned.1.call-update) | async-done | bytes 400
  709.0 1.4 copy.101
  710.4 58.7 %reduce-scatter.29.cloned.1.call-done = f32[96,128]{1,0:T(8,128)} async-done(((f32[1536,128]{1,0:T(8,128)}), f32[96,128]{1,0:T(8,128)}) %reduce-scatter.29.cloned.1.call-update) | async-done | bytes 49168 | tf_op jit(solution)/shard_map/reduce_scatter | solution.py:314
  769.1 59.8 %reduce-scatter.27.cloned.1.call-done = f32[96,128]{1,0:T(8,128)} async-done(((f32[1536,128]{1,0:T(8,128)}), f32[96,128]{1,0:T(8,128)}) %reduce-scatter.27.cloned.1.call-update) | async-done | bytes 49168 | tf_op jit(solution)/shard_map/reduce_scatter | solution.py:313
  828.9 79.1 %reduce-scatter.25.cloned.1.call-done = f32[96,768]{1,0:T(8,128)} async-done(((f32[1536,768]{1,0:T(8,128)}), f32[96,768]{1,0:T(8,128)}) %reduce-scatter.25.cloned.1.call-update) | async-done | bytes 294928 | tf_op jit(solution)/shard_map/reduce_scatter | solution.py:312
  908.0 79.1 %reduce-scatter.31.cloned.1.call-done = f32[768,96]{0,1:T(8,128)} async-done(((f32[768,1536]{0,1:T(8,128)}), f32[768,96]{0,1:T(8,128)}) %reduce-scatter.31.cloned.1.call-update) | async-done | bytes 294928 | tf_op jit(solution)/shard_map/reduce_scatter | solution.py:315
  987.1 268.5 %reduce-scatter.33.cloned.1.call-done = f32[96,4480]{1,0:T(8,128)} async-done(((f32[1536,4480]{1,0:T(8,128)}), f32[96,4480]{1,0:T(8,128)}) %reduce-scatter.33.cloned.1.call-update) | async-done | bytes 1720336 | tf_op jit(solution)/shard_map/reduce_scatter | solution.py:284
  1255.6 268.4 %reduce-scatter.35.cloned.1.call-done = f32[96,4480]{1,0:T(8,128)} async-done(((f32[1536,4480]{1,0:T(8,128)}), f32[96,4480]{1,0:T(8,128)}) %reduce-scatter.35.cloned.1.call-update) | async-done | bytes 1720336 | tf_op jit(solution)/shard_map/reduce_scatter | solution.py:285
  1524.0 268.4 %reduce-scatter.37.cloned.1.call-done = f32[4480,96]{0,1:T(8,128)} async-done(((f32[4480,1536]{0,1:T(8,128)}), f32[4480,96]{0,1:T(8,128)}) %reduce-scatter.37.cloned.1.call-update) | async-done | bytes 1720336 | tf_op jit(solution)/shard_map/reduce_scatter | solution.py:286
  (166 shorter events, 26.6 us)
Async XLA Ops:
  7.2 100.5 %copy-start.33 = (bf16[1,96,128]{2,1,0:T(8,128)(2,1)S(1)}, bf16[1,96,128]{2,1,0:T(8,128)(2,1)}, u32[]{:S(2)}) copy-start(bf16[1,96,128]{2,1,0:T(8,128)(2,1)} %param.21) | copy-start | bytes 73732
  7.2 121.5 %all-gather.18.cloned.1.call-start = ((), (), s32[]{:S(2)}) async-start(), calls=%async_computation.23 | async-start | bytes 2506752 | tf_op jit(solution)/shard_map/all_gather | solution.py:221
  7.9 127.3 %all-gather.20.cloned.1.call-start = ((), (), s32[]{:S(2)}) async-start(), calls=%async_computation.24 | async-start | bytes 2506752 | tf_op jit(solution)/shard_map/all_gather | solution.py:224
  8.7 154.9 %reduce-scatter.17.cloned.1.call-start = ((), (), s32[]{:S(2)}) async-start(), calls=%async_computation.12 | async-start | bytes 1179648 | tf_op jit(solution)/shard_map/reduce_scatter | solution.py:243
  12.0 115.3 %copy-start.34 = (f32[1,256]{1,0:T(1,128)}, f32[1,256]{1,0:T(1,128)S(1)}, u32[]{:S(2)}) copy-start(f32[1,256]{1,0:T(1,128)S(1)} %convert_element_type.156) | copy-start | bytes 3076
  70.0 57.3 %copy-start.37 = (f32[64]{0:T(128)}, f32[64]{0:T(128)S(1)}, u32[]{:S(2)}) copy-start(f32[64]{0:T(128)S(1)} %multiply_exponential_fusion) | copy-start | bytes 772
  92.9 13.8 copy-start.7
  92.9 0.6 copy-start.39
  94.7 33.8 %copy-start.40 = (s32[1,256]{1,0:T(1,128)S(1)}, s32[1,256]{1,0:T(1,128)}, u32[]{:S(2)}) copy-start(s32[1,256]{1,0:T(1,128)} %param.17) | copy-start | bytes 3076
  125.9 5.2 copy-start.5
  131.7 2.2 copy-start.25
  131.7 2.2 copy-start.27
  132.0 2.6 copy-start.29
  133.2 0.7 copy-start.11
  133.2 1.8 copy-start.9
  134.6 0.6 copy-start.32
  135.2 4.1 copy-start.20
  138.7 24.9 %copy-start = (bf16[128,1536]{1,0:T(8,128)(2,1)S(1)}, bf16[128,1536]{1,0:T(8,128)(2,1)}, u32[]{:S(2)}) copy-start(bf16[128,1536]{1,0:T(8,128)(2,1)} %param.15) | copy-start | bytes 1179652
  138.7 134.1 %all-gather.24.cloned.1.call-start = ((), (), s32[]{:S(2)}) async-start(), calls=%async_computation.26 | async-start | bytes 14622720 | tf_op jit(solution)/shard_map/all_gather | solution.py:234
  139.3 241.5 %all-gather.26.cloned.1.call-start = ((), (), s32[]{:S(2)}) async-start(), calls=%async_computation.27 | async-start | bytes 14622720 | tf_op jit(solution)/shard_map/all_gather | solution.py:235
  139.9 349.0 %all-gather.22.cloned.1.call-start = ((), (), s32[]{:S(2)}) async-start(), calls=%async_computation.25 | async-start | bytes 14622720 | tf_op jit(solution)/shard_map/all_gather | solution.py:233
  140.5 395.8 %reduce-scatter.21.cloned.1.call-start = ((), (), s32[]{:S(2)}) async-start(), calls=%async_computation.14 | async-start | bytes 1179648 | tf_op jit(solution)/shard_map/reduce_scatter | solution.py:243
  164.8 0.6 copy-start.36
  503.4 8.7 copy-start.17
  503.4 8.7 copy-start.18
  512.1 24.2 %copy-start.1 = (bf16[128,1536]{1,0:T(8,128)(2,1)S(1)}, bf16[128,1536]{1,0:T(8,128)(2,1)}, u32[]{:S(2)}) copy-start(bf16[128,1536]{1,0:T(8,128)(2,1)} %reduce-scatter.17.cloned.1.call-done) | copy-start | bytes 1179652
  520.4 67.0 %reduce-scatter.23.cloned.1.call-start = ((), (), s32[]{:S(2)}) async-start(), calls=%async_computation.15 | async-start | bytes 1179648 | tf_op jit(solution)/shard_map/reduce_scatter | solution.py:243
  536.2 16.5 copy-start.42
  538.4 0.5 copy-start.41
  551.9 0.9 copy-start.14
  556.2 2.7 copy-start.4
  556.2 2.7 copy-start.30
  556.2 2.7 copy-start.31
  559.3 1.0 copy-start.10
  559.3 1.1 copy-start.12
  559.3 1.7 copy-start.26
  559.3 1.7 copy-start.28
  560.4 1.0 copy-start.35
  560.4 1.0 copy-start.38
  560.4 2.0 copy-start.19
  564.9 2.6 copy-start.6
  564.9 2.6 copy-start.22
  564.9 2.6 copy-start.23
  567.5 1.0 copy-start.8
  567.5 1.0 copy-start.24
  569.8 115.4 %reduce-scatter.19.cloned.1.call-start = ((), (), s32[]{:S(2)}) async-start(), calls=%async_computation.13 | async-start | bytes 1179648 | tf_op jit(solution)/shard_map/reduce_scatter | solution.py:243
  580.2 128.9 %reduce-scatter.39.cloned.1.call-start = ((), (), s32[]{:S(2)}) async-start(), calls=%async_computation.28 | async-start | bytes 811008
  593.0 176.1 %reduce-scatter.29.cloned.1.call-start = ((), (), s32[]{:S(2)}) async-start(), calls=%async_computation.18 | async-start | bytes 835584 | tf_op jit(solution)/shard_map/reduce_scatter | solution.py:314
  595.5 233.4 %reduce-scatter.27.cloned.1.call-start = ((), (), s32[]{:S(2)}) async-start(), calls=%async_computation.17 | async-start | bytes 835584 | tf_op jit(solution)/shard_map/reduce_scatter | solution.py:313
  597.8 310.2 %reduce-scatter.25.cloned.1.call-start = ((), (), s32[]{:S(2)}) async-start(), calls=%async_computation.16 | async-start | bytes 5013504 | tf_op jit(solution)/shard_map/reduce_scatter | solution.py:312
  600.8 1.1 copy-start.15
  600.8 1.2 copy-start.21
  600.8 386.3 %reduce-scatter.31.cloned.1.call-start = ((), (), s32[]{:S(2)}) async-start(), calls=%async_computation.19 | async-start | bytes 5013504 | tf_op jit(solution)/shard_map/reduce_scatter | solution.py:315
  605.0 1.1 copy-start.3
  605.0 650.6 %reduce-scatter.33.cloned.1.call-start = ((), (), s32[]{:S(2)}) async-start(), calls=%async_computation.20 | async-start | bytes 29245440 | tf_op jit(solution)/shard_map/reduce_scatter | solution.py:284
  619.0 905.1 %reduce-scatter.35.cloned.1.call-start = ((), (), s32[]{:S(2)}) async-start(), calls=%async_computation.21 | async-start | bytes 29245440 | tf_op jit(solution)/shard_map/reduce_scatter | solution.py:285
  631.9 1.1 copy-start.16
  632.0 1160.5 %reduce-scatter.37.cloned.1.call-start = ((), (), s32[]{:S(2)}) async-start(), calls=%async_computation.22 | async-start | bytes 29245440 | tf_op jit(solution)/shard_map/reduce_scatter | solution.py:286
  646.0 39.2 %copy-start.13 = (bf16[128,1536]{1,0:T(8,128)(2,1)S(1)}, bf16[128,1536]{1,0:T(8,128)(2,1)}, u32[]{:S(2)}) copy-start(bf16[128,1536]{1,0:T(8,128)(2,1)} %reduce-scatter.21.cloned.1.call-done) | copy-start | bytes 1179652
  646.1 39.1 %copy-start.2 = (f32[128,1536]{1,0:T(8,128)S(1)}, f32[128,1536]{1,0:T(8,128)}, u32[]{:S(2)}) copy-start(f32[128,1536]{1,0:T(8,128)} %param.16) | copy-start | bytes 2359300
Sparse Core Ops, SparseCore 0:
  10.3 45.3 all-gather.17
  57.9 41.1 all-gather.19
  138.8 24.7 reduce-scatter.16
  165.8 107.0 all-gather.23
  275.0 105.8 all-gather.25
  383.0 105.8 all-gather.21
  520.5 15.6 reduce-scatter.20
  569.9 17.5 reduce-scatter.22
  590.3 17.4 reduce-scatter.18
  612.8 96.2 reduce-scatter.38
  713.2 55.9 reduce-scatter.28
  773.1 55.7 reduce-scatter.26
  833.4 74.5 reduce-scatter.24
  912.3 74.8 reduce-scatter.30
  991.7 263.9 reduce-scatter.32
  1260.2 263.8 reduce-scatter.34
  1528.6 263.8 reduce-scatter.36
where the time goes:
time: 1810 us; the launch traced here: 1800 us
  waiting for transfers between devices  1420 us (78%)
  blocking collectives  184 us (10%)
  matrix products  131 us (7%)
  other arithmetic  26.2 us (1%)
  local copies, waits for them, and re-layouts  24.6 us (1%)
    reduce_scatter x1, waiting for transfers between devices, per_device(): lax.psum_scatter(mlp_grads[0], 'dp', scatter_dimension=0, tiled=True)  268 us
    reduce_scatter x1, waiting for transfers between devices, per_device(): lax.psum_scatter(mlp_grads[1], 'dp', scatter_dimension=0, tiled=True)  268 us
    reduce_scatter x1, waiting for transfers between devices, per_device(): lax.psum_scatter(mlp_grads[2], 'dp', scatter_dimension=1, tiled=True)  268 us
    all_gather x1, waiting for transfers between devices, fetch_mlp(): lax.all_gather(gate_weight[layer_no], 'dp', axis=0, tiled=True)  97 us
    all_gather x1, waiting for transfers between devices, fetch_mlp(): lax.all_gather(down_weight[layer_no], 'dp', axis=1, tiled=True)  96.9 us
    all_gather x1, waiting for transfers between devices, fetch_mlp(): lax.all_gather(up_weight[layer_no], 'dp', axis=0, tiled=True)  94.6 us
    reduce_scatter x1, waiting for transfers between devices, per_device(): lax.psum_scatter(spread_grads[3], 'dp', scatter_dimension=1, tiled=True)  79.1 us
    reduce_scatter x1, waiting for transfers between devices, per_device(): lax.psum_scatter(spread_grads[0], 'dp', scatter_dimension=0, tiled=True)  79.1 us
  transfers between devices with their start and end apart: 17, of which 14 were waited for; matrix products, arithmetic and copies ran while one was open for 7% of the time, Pallas kernels for 0%

commit v1 on v0

--- a/solution.py
+++ b/solution.py
@@ -7,6 +7,23 @@
 LAYERS = 1
 eps = 1e-06
 theta_log = 13.815510557964274
+
+
+def in_order(pieces, dim):
+    shape = list(pieces.shape[1:])
+    shape[dim] *= pieces.shape[0]
+    return jnp.moveaxis(pieces, 0, dim).reshape(shape)
+
+
+def collect(x, axis, dim):
+    size = lax.axis_size(axis)
+    right = [(i, (i + 1) % size) for i in range(size)]
+    parts = [x]
+    while len(parts) < size:
+        parts.append(lax.ppermute(parts[-1], axis, right))
+    index = lax.axis_index(axis)
+    parts = jnp.stack(parts)[(index - jnp.arange(size)) % size]
+    return in_order(parts, dim)
 
 
 def product(form, left, right):
@@ -231,7 +248,7 @@
     def fetch_mlp(layer_no):
         return (
             lax.all_gather(gate_weight[layer_no], "dp", axis=0, tiled=True),
-            lax.all_gather(up_weight[layer_no], "dp", axis=0, tiled=True),
+            collect(up_weight[layer_no], "dp", 0),
             lax.all_gather(down_weight[layer_no], "dp", axis=1, tiled=True),
             lax.all_gather(norm_gains[layer_no, 1], "dp", axis=0, tiled=True),
         )

time: 1810 us -> 1850 us (1.022)
  local copies, waits for them, and re-layouts: 24.6 us -> 55 us
    ppermute x0 -> x15, waiting for transfers between devices: none -> 305 us  [collect(): parts.append(lax.ppermute(parts[-1], axis, right))]
    all_gather x1, waiting for transfers between devices: 97 us -> 0.01 us  [fetch_mlp(): lax.all_gather(gate_weight[layer_no], 'dp', axis=0, tiled=True)]
    all_gather x1, waiting for transfers between devices: 96.9 us -> 0.01 us  [fetch_mlp(): lax.all_gather(down_weight[layer_no], 'dp', axis=1, tiled=True)]
    all_gather x1 -> x0, waiting for transfers between devices: 94.6 us -> none  [fetch_mlp(): lax.all_gather(up_weight[layer_no], 'dp', axis=0, tiled=True)]
  transfers between devices with their start and end apart: 17 -> 31, of which waited for: 14 -> 24; matrix products, arithmetic and copies ran while one was open for 7% -> 8% of each run, Pallas kernels for 0% -> 0%
where the time goes in v1:
time: 1850 us; the launch traced here: 1840 us
  waiting for transfers between devices  1430 us (77%)
  blocking collectives  180 us (10%)
  matrix products  128 us (7%)
  local copies, waits for them, and re-layouts  55 us (3%)
  other arithmetic  27.8 us (2%)
    ppermute x15, waiting for transfers between devices, collect(): parts.append(lax.ppermute(parts[-1], axis, right))  305 us
    reduce_scatter x1, waiting for transfers between devices, per_device(): lax.psum_scatter(mlp_grads[0], 'dp', scatter_dimension=0, tiled=True)  269 us
    reduce_scatter x1, waiting for transfers between devices, per_device(): lax.psum_scatter(mlp_grads[2], 'dp', scatter_dimension=1, tiled=True)  268 us
    reduce_scatter x1, waiting for transfers between devices, per_device(): lax.psum_scatter(mlp_grads[1], 'dp', scatter_dimension=0, tiled=True)  268 us
    reduce_scatter x1, waiting for transfers between devices, per_device(): lax.psum_scatter(spread_grads[3], 'dp', scatter_dimension=1, tiled=True)  79.2 us
    reduce_scatter x1, waiting for transfers between devices, per_device(): lax.psum_scatter(spread_grads[0], 'dp', scatter_dimension=0, tiled=True)  78.9 us
    unnamed x2, blocking collectives  71.4 us
    reduce_scatter x1, waiting for transfers between devices, per_device(): lax.psum_scatter(spread_grads[2], 'dp', scatter_dimension=0, tiled=True)  59.9 us
  transfers between devices with their start and end apart: 31, of which 24 were waited for; matrix products, arithmetic and copies ran while one was open for 8% of the time, Pallas kernels for 0%

profile of v1, /device:TPU:0, one launch (start us, length us, event | category | flops | bytes accessed | tf_op | source)
XLA Modules:
  0.0 1839.3 jit_solution(1008463641297857062)
XLA Ops:
  14.3 37.1 %all-reduce.7 = (bf16[1536]{0:T(1024)(128)(2,1)S(1)}, bf16[128]{0:T(256)(128)(2,1)S(1)}, bf16[128]{0:T(256)(128)(2,1)S(1)}, bf16[1536]{0:T(1024)(128)(2,1)}) all-reduce(bf16[1536]{0:T(1024)(128)(2,1)S(1)} %dynamic-update-slice, bf16[128]{0:T(256)(128)(2,1)S(1)} %dynamic-update-slice.1, ...), channel_id=2, replica_groups=mesh['dp'=16,'tensor'=2] {'dp'}, use_global_device_ids=true, to_apply=%add | all-reduce | flops 3328 | bytes 13312
  52.2 17.4 all-gather.6
  71.5 21.4 %all-gather.1 = bf16[1,1536,128]{2,1,0:T(8,128)(2,1)S(1)} all-gather(bf16[1,96,128]{2,1,0:T(8,128)(2,1)} %param.22), channel_id=3, replica_groups=mesh['dp'=16,'tensor'=2] {'dp'}, dimensions={1}, use_global_device_ids=true | all-gather | bytes 417792 | tf_op jit(solution)/shard_map/all_gather | solution.py:240
  94.8 12.0 all_gather.54
  107.9 18.2 all-gather.3
  128.8 2.4 fusion.27
  136.8 3.5 convolution_convert_fusion
  144.4 19.6 %all_gather.66 = bf16[256,1536]{1,0:T(8,128)(2,1)} all-gather(bf16[128,1536]{1,0:T(8,128)(2,1)S(1)} %convert_element_type.173), channel_id=1, replica_groups=mesh['dp'=16,'tensor'=2] {'tensor'}, dimensions={0}, use_global_device_ids=true | all-gather | bytes 1179648 | tf_op jit(solution)/shard_map/all_gather | solution.py:257
  164.0 2.1 constant_dynamic-update-slice_fusion
  166.3 2.2 bitcast_dynamic-update-slice_fusion.14
  168.4 13.0 collective-permute-done.1
  183.0 31.9 %collective-permute-done.2 = bf16[96,4480]{1,0:T(8,128)(2,1)S(1)} collective-permute-done((bf16[96,4480]{1,0:T(8,128)(2,1)S(1)}, bf16[96,4480]{1,0:T(8,128)(2,1)S(1)}, u32[]{:S(2)}, u32[]{:S(2)}) %collective-permute-start.2) | collective-permute-done | bytes 860192 | tf_op jit(solution)/shard_map/ppermute | solution.py:23
  215.9 21.9 %collective-permute-done.3 = bf16[96,4480]{1,0:T(8,128)(2,1)S(1)} collective-permute-done((bf16[96,4480]{1,0:T(8,128)(2,1)S(1)}, bf16[96,4480]{1,0:T(8,128)(2,1)S(1)}, u32[]{:S(2)}, u32[]{:S(2)}) %collective-permute-start.3) | collective-permute-done | bytes 860192 | tf_op jit(solution)/shard_map/ppermute | solution.py:23
  238.7 32.5 %collective-permute-done.4 = bf16[96,4480]{1,0:T(8,128)(2,1)S(1)} collective-permute-done((bf16[96,4480]{1,0:T(8,128)(2,1)S(1)}, bf16[96,4480]{1,0:T(8,128)(2,1)S(1)}, u32[]{:S(2)}, u32[]{:S(2)}) %collective-permute-start.4) | collective-permute-done | bytes 860192 | tf_op jit(solution)/shard_map/ppermute | solution.py:23
  272.2 31.7 %collective-permute-done.5 = bf16[96,4480]{1,0:T(8,128)(2,1)} collective-permute-done((bf16[96,4480]{1,0:T(8,128)(2,1)S(1)}, bf16[96,4480]{1,0:T(8,128)(2,1)}, u32[]{:S(2)}, u32[]{:S(2)}) %collective-permute-start.5) | collective-permute-done | bytes 860192 | tf_op jit(solution)/shard_map/ppermute | solution.py:23
  303.8 2.2 bitcast_dynamic-update-slice_fusion.9
  308.4 8.6 all_gather.63
  316.9 2.3 collective-permute-done.6
  319.2 2.1 bitcast_dynamic-update-slice_fusion.8
  321.3 31.5 %collective-permute-done.7 = bf16[96,4480]{1,0:T(8,128)(2,1)S(1)} collective-permute-done((bf16[96,4480]{1,0:T(8,128)(2,1)}, bf16[96,4480]{1,0:T(8,128)(2,1)S(1)}, u32[]{:S(2)}, u32[]{:S(2)}) %collective-permute-start.7) | collective-permute-done | bytes 860192 | tf_op jit(solution)/shard_map/ppermute | solution.py:23
  353.9 20.2 %collective-permute-done.8 = bf16[96,4480]{1,0:T(8,128)(2,1)S(1)} collective-permute-done((bf16[96,4480]{1,0:T(8,128)(2,1)S(1)}, bf16[96,4480]{1,0:T(8,128)(2,1)S(1)}, u32[]{:S(2)}, u32[]{:S(2)}) %collective-permute-start.8) | collective-permute-done | bytes 860192 | tf_op jit(solution)/shard_map/ppermute | solution.py:23
  375.0 32.5 %collective-permute-done.9 = bf16[96,4480]{1,0:T(8,128)(2,1)S(1)} collective-permute-done((bf16[96,4480]{1,0:T(8,128)(2,1)S(1)}, bf16[96,4480]{1,0:T(8,128)(2,1)S(1)}, u32[]{:S(2)}, u32[]{:S(2)}) %collective-permute-start.9) | collective-permute-done | bytes 860192 | tf_op jit(solution)/shard_map/ppermute | solution.py:23
  408.5 32.2 %collective-permute-done.10 = bf16[96,4480]{1,0:T(8,128)(2,1)S(1)} collective-permute-done((bf16[96,4480]{1,0:T(8,128)(2,1)S(1)}, bf16[96,4480]{1,0:T(8,128)(2,1)S(1)}, u32[]{:S(2)}, u32[]{:S(2)}) %collective-permute-start.10) | collective-permute-done | bytes 860192 | tf_op jit(solution)/shard_map/ppermute | solution.py:23
  441.7 13.9 collective-permute-done.11
  456.6 13.9 collective-permute-done.12
  471.4 14.0 collective-permute-done.13
  486.8 13.9 collective-permute-done.14
  501.7 12.0 gather_fusion
  513.7 11.1 fusion
  524.7 11.2 fusion.6
  535.9 9.4 multiply_convert_fusion
  545.4 8.5 fusion.4
  553.9 8.3 fusion.11
  563.7 12.0 reduce-scatter.21.cloned.1.call-done
  575.7 2.1 fusion.50
  578.4 1.6 fusion.107
  580.0 11.4 all_gather.67
  592.3 1.5 fusion.31
  593.8 1.9 copy.80
  595.7 1.5 fusion.20
  600.2 1.6 fusion.110
  605.6 2.5 fusion.16
  610.0 10.3 fusion.8
  621.7 5.9 reduce-scatter.23.cloned.1.call-done
  627.6 1.9 fusion.55
  630.7 2.4 copy.100
  633.2 2.2 fusion.96
  635.5 2.2 fusion.89
  637.8 3.0 fusion.111
  642.0 3.0 fusion.112
  646.0 12.8 fusion.113
  659.0 12.9 fusion.114
  673.0 12.9 fusion.115
  686.7 1.5 fusion.72
  689.1 34.3 %all-reduce.6 = (f32[6,128]{1,0:T(8,128)S(1)}, f32[1,1,128]{2,1,0:T(1,128)}, f32[1,128]{1,0:T(1,128)S(1)}) all-reduce(f32[6,128]{1,0:T(8,128)} %fusion.70, f32[1,1,128]{2,1,0:T(1,128)} %bitcast.269, f32[1,128]{1,0:T(1,128)} %bitcast.268), channel_id=22, replica_groups=mesh['dp'=16,'tensor'=2] {'dp'}, use_global_device_ids=true, to_apply=%region_18.19.clone | all-reduce | flops 1024 | bytes 8192
  725.3 2.8 fusion.46
  728.1 21.3 %reduce-scatter.39.cloned.1.call-done = f32[48,2]{1,0:T(8,128)} async-done(((f32[1536,2]{1,0:T(8,128)}), f32[48,2]{1,0:T(8,128)}) %reduce-scatter.39.cloned.1.call-update) | async-done | bytes 400
  750.8 58.4 %reduce-scatter.27.cloned.1.call-done = f32[96,128]{1,0:T(8,128)} async-done(((f32[1536,128]{1,0:T(8,128)}), f32[96,128]{1,0:T(8,128)}) %reduce-scatter.27.cloned.1.call-update) | async-done | bytes 49168 | tf_op jit(solution)/shard_map/reduce_scatter | solution.py:330
  809.2 59.9 %reduce-scatter.29.cloned.1.call-done = f32[96,128]{1,0:T(8,128)} async-done(((f32[1536,128]{1,0:T(8,128)}), f32[96,128]{1,0:T(8,128)}) %reduce-scatter.29.cloned.1.call-update) | async-done | bytes 49168 | tf_op jit(solution)/shard_map/reduce_scatter | solution.py:331
  869.1 78.9 %reduce-scatter.25.cloned.1.call-done = f32[96,768]{1,0:T(8,128)} async-done(((f32[1536,768]{1,0:T(8,128)}), f32[96,768]{1,0:T(8,128)}) %reduce-scatter.25.cloned.1.call-update) | async-done | bytes 294928 | tf_op jit(solution)/shard_map/reduce_scatter | solution.py:329
  948.0 79.2 %reduce-scatter.31.cloned.1.call-done = f32[768,96]{0,1:T(8,128)} async-done(((f32[768,1536]{0,1:T(8,128)}), f32[768,96]{0,1:T(8,128)}) %reduce-scatter.31.cloned.1.call-update) | async-done | bytes 294928 | tf_op jit(solution)/shard_map/reduce_scatter | solution.py:332
  1027.2 268.5 %reduce-scatter.33.cloned.1.call-done = f32[96,4480]{1,0:T(8,128)} async-done(((f32[1536,4480]{1,0:T(8,128)}), f32[96,4480]{1,0:T(8,128)}) %reduce-scatter.33.cloned.1.call-update) | async-done | bytes 1720336 | tf_op jit(solution)/shard_map/reduce_scatter | solution.py:301
  1295.8 268.4 %reduce-scatter.35.cloned.1.call-done = f32[96,4480]{1,0:T(8,128)} async-done(((f32[1536,4480]{1,0:T(8,128)}), f32[96,4480]{1,0:T(8,128)}) %reduce-scatter.35.cloned.1.call-update) | async-done | bytes 1720336 | tf_op jit(solution)/shard_map/reduce_scatter | solution.py:302
  1564.2 268.4 %reduce-scatter.37.cloned.1.call-done = f32[4480,96]{0,1:T(8,128)} async-done(((f32[4480,1536]{0,1:T(8,128)}), f32[4480,96]{0,1:T(8,128)}) %reduce-scatter.37.cloned.1.call-update) | async-done | bytes 1720336 | tf_op jit(solution)/shard_map/reduce_scatter | solution.py:303
  (202 shorter events, 60.6 us)
Async XLA Ops:
  7.2 100.7 %copy-start.30 = (bf16[1,96,128]{2,1,0:T(8,128)(2,1)S(1)}, bf16[1,96,128]{2,1,0:T(8,128)(2,1)}, u32[]{:S(2)}) copy-start(bf16[1,96,128]{2,1,0:T(8,128)(2,1)} %param.21) | copy-start | bytes 73732
  7.2 121.5 %copy-start.35 = (s32[1,256]{1,0:T(1,128)S(1)}, s32[1,256]{1,0:T(1,128)}, u32[]{:S(2)}) copy-start(s32[1,256]{1,0:T(1,128)} %param.17) | copy-start | bytes 3076
  7.2 121.6 %all-gather.16.cloned.1.call-start = ((), (), s32[]{:S(2)}) async-start(), calls=%async_computation.23 | async-start | bytes 2506752 | tf_op jit(solution)/shard_map/all_gather | solution.py:238
  7.9 128.8 %all-gather.18.cloned.1.call-start = ((), (), s32[]{:S(2)}) async-start(), calls=%async_computation.24 | async-start | bytes 2506752 | tf_op jit(solution)/shard_map/all_gather | solution.py:241
  8.7 297.3 %reduce-scatter.17.cloned.1.call-start = ((), (), s32[]{:S(2)}) async-start(), calls=%async_computation.12 | async-start | bytes 1179648 | tf_op jit(solution)/shard_map/reduce_scatter | solution.py:260
  70.3 60.9 %copy-start.31 = (f32[1,256]{1,0:T(1,128)}, f32[1,256]{1,0:T(1,128)S(1)}, u32[]{:S(2)}) copy-start(f32[1,256]{1,0:T(1,128)S(1)} %convert_element_type.156) | copy-start | bytes 3076
  70.4 58.4 %copy-start.33 = (f32[64]{0:T(128)}, f32[64]{0:T(128)S(1)}, u32[]{:S(2)}) copy-start(f32[64]{0:T(128)S(1)} %multiply_exponential_fusion) | copy-start | bytes 772
  93.0 13.9 copy-start.9
  126.1 5.5 copy-start.7
  133.3 7.0 copy-start.11
  135.4 4.8 copy-start.29
  136.7 29.4 %copy-start.21 = (bf16[128,6,256]{2,0,1:T(8,128)(2,1)}, bf16[128,6,256]{2,0,1:T(8,128)(2,1)S(1)}, u32[]{:S(2)}) copy-start(bf16[128,6,256]{2,0,1:T(8,128)(2,1)S(1)} %convolution_convert_fusion.1) | copy-start | bytes 1179652
  140.3 373.4 %all-gather.22.cloned.1.call-start = ((), (), s32[]{:S(2)}) async-start(), calls=%async_computation.26 | async-start | bytes 14622720 | tf_op jit(solution)/shard_map/all_gather | solution.py:252
  140.9 383.8 %all-gather.20.cloned.1.call-start = ((), (), s32[]{:S(2)}) async-start(), calls=%async_computation.25 | async-start | bytes 14622720 | tf_op jit(solution)/shard_map/all_gather | solution.py:250
  141.5 434.2 %reduce-scatter.21.cloned.1.call-start = ((), (), s32[]{:S(2)}) async-start(), calls=%async_computation.14 | async-start | bytes 1179648 | tf_op jit(solution)/shard_map/reduce_scatter | solution.py:260
  141.5 24.6 %collective-permute-start = (bf16[96,4480]{1,0:T(8,128)(2,1)}, bf16[96,4480]{1,0:T(8,128)(2,1)}, u32[]{:S(2)}, u32[]{:S(2)}) collective-permute-start(bf16[96,4480]{1,0:T(8,128)(2,1)} %bitcast.262), channel_id=1, source_target_pairs={{0,2},{2,4},{4,6},{6,8},{8,10},{10,12},{12,14},{14,16},{16,18},{18... | collective-permute-start | bytes 2580488 | tf_op jit(solution)/shard_map/ppermute | solution.py:23
  166.2 15.3 collective-permute-start.1
  168.4 137.5 %copy-start = (bf16[128,1536]{1,0:T(8,128)(2,1)S(1)}, bf16[128,1536]{1,0:T(8,128)(2,1)}, u32[]{:S(2)}) copy-start(bf16[128,1536]{1,0:T(8,128)(2,1)} %param.15) | copy-start | bytes 1179652
  181.4 33.5 %collective-permute-start.2 = (bf16[96,4480]{1,0:T(8,128)(2,1)S(1)}, bf16[96,4480]{1,0:T(8,128)(2,1)S(1)}, u32[]{:S(2)}, u32[]{:S(2)}) collective-permute-start(bf16[96,4480]{1,0:T(8,128)(2,1)S(1)} %collective-permute-done.1), channel_id=1, source_target_pairs={{0,2},{2,4},{4,6},{6,8},{8,10},{10,12},{12,14},{14,16},{16,18},{18... | collective-permute-start | bytes 2580488 | tf_op jit(solution)/shard_map/ppermute | solution.py:23
  214.9 22.8 %collective-permute-start.3 = (bf16[96,4480]{1,0:T(8,128)(2,1)S(1)}, bf16[96,4480]{1,0:T(8,128)(2,1)S(1)}, u32[]{:S(2)}, u32[]{:S(2)}) collective-permute-start(bf16[96,4480]{1,0:T(8,128)(2,1)S(1)} %collective-permute-done.2), channel_id=1, source_target_pairs={{0,2},{2,4},{4,6},{6,8},{8,10},{10,12},{12,14},{14,16},{16,18},{18... | collective-permute-start | bytes 2580488 | tf_op jit(solution)/shard_map/ppermute | solution.py:23
  237.7 33.5 %collective-permute-start.4 = (bf16[96,4480]{1,0:T(8,128)(2,1)S(1)}, bf16[96,4480]{1,0:T(8,128)(2,1)S(1)}, u32[]{:S(2)}, u32[]{:S(2)}) collective-permute-start(bf16[96,4480]{1,0:T(8,128)(2,1)S(1)} %collective-permute-done.3), channel_id=1, source_target_pairs={{0,2},{2,4},{4,6},{6,8},{8,10},{10,12},{12,14},{14,16},{16,18},{18... | collective-permute-start | bytes 2580488 | tf_op jit(solution)/shard_map/ppermute | solution.py:23
  271.2 32.6 %collective-permute-start.5 = (bf16[96,4480]{1,0:T(8,128)(2,1)S(1)}, bf16[96,4480]{1,0:T(8,128)(2,1)}, u32[]{:S(2)}, u32[]{:S(2)}) collective-permute-start(bf16[96,4480]{1,0:T(8,128)(2,1)S(1)} %collective-permute-done.4), channel_id=1, source_target_pairs={{0,2},{2,4},{4,6},{6,8},{8,10},{10,12},{12,14},{14,16},{16,18},{18... | collective-permute-start | bytes 2580488 | tf_op jit(solution)/shard_map/ppermute | solution.py:23
  303.8 15.4 collective-permute-start.6
  307.2 9.7 copy-start.32
  319.2 33.7 %collective-permute-start.7 = (bf16[96,4480]{1,0:T(8,128)(2,1)}, bf16[96,4480]{1,0:T(8,128)(2,1)S(1)}, u32[]{:S(2)}, u32[]{:S(2)}) collective-permute-start(bf16[96,4480]{1,0:T(8,128)(2,1)} %collective-permute-done.6), channel_id=1, source_target_pairs={{0,2},{2,4},{4,6},{6,8},{8,10},{10,12},{12,14},{14,16},{16,18},{18... | collective-permute-start | bytes 2580488 | tf_op jit(solution)/shard_map/ppermute | solution.py:23
  352.9 21.2 %collective-permute-start.8 = (bf16[96,4480]{1,0:T(8,128)(2,1)S(1)}, bf16[96,4480]{1,0:T(8,128)(2,1)S(1)}, u32[]{:S(2)}, u32[]{:S(2)}) collective-permute-start(bf16[96,4480]{1,0:T(8,128)(2,1)S(1)} %collective-permute-done.7), channel_id=1, source_target_pairs={{0,2},{2,4},{4,6},{6,8},{8,10},{10,12},{12,14},{14,16},{16,18},{18... | collective-permute-start | bytes 2580488 | tf_op jit(solution)/shard_map/ppermute | solution.py:23
  374.1 33.5 %collective-permute-start.9 = (bf16[96,4480]{1,0:T(8,128)(2,1)S(1)}, bf16[96,4480]{1,0:T(8,128)(2,1)S(1)}, u32[]{:S(2)}, u32[]{:S(2)}) collective-permute-start(bf16[96,4480]{1,0:T(8,128)(2,1)S(1)} %collective-permute-done.8), channel_id=1, source_target_pairs={{0,2},{2,4},{4,6},{6,8},{8,10},{10,12},{12,14},{14,16},{16,18},{18... | collective-permute-start | bytes 2580488 | tf_op jit(solution)/shard_map/ppermute | solution.py:23
  407.5 33.2 %collective-permute-start.10 = (bf16[96,4480]{1,0:T(8,128)(2,1)S(1)}, bf16[96,4480]{1,0:T(8,128)(2,1)S(1)}, u32[]{:S(2)}, u32[]{:S(2)}) collective-permute-start(bf16[96,4480]{1,0:T(8,128)(2,1)S(1)} %collective-permute-done.9), channel_id=1, source_target_pairs={{0,2},{2,4},{4,6},{6,8},{8,10},{10,12},{12,14},{14,16},{16,18},{18... | collective-permute-start | bytes 2580488 | tf_op jit(solution)/shard_map/ppermute | solution.py:23
  440.7 14.9 collective-permute-start.11
  455.6 14.9 collective-permute-start.12
  470.5 14.9 collective-permute-start.13
  485.4 15.3 collective-permute-start.14
  524.7 11.2 copy-start.1
  524.7 11.2 copy-start.4
  545.3 8.5 copy-start.19
  553.9 21.8 %copy-start.2 = (bf16[128,1536]{1,0:T(8,128)(2,1)S(1)}, bf16[128,1536]{1,0:T(8,128)(2,1)}, u32[]{:S(2)}) copy-start(bf16[128,1536]{1,0:T(8,128)(2,1)} %reduce-scatter.17.cloned.1.call-done) | copy-start | bytes 1179652
  562.2 65.4 %reduce-scatter.23.cloned.1.call-start = ((), (), s32[]{:S(2)}) async-start(), calls=%async_computation.15 | async-start | bytes 1179648 | tf_op jit(solution)/shard_map/reduce_scatter | solution.py:260
  575.7 16.6 copy-start.37
  595.7 2.8 copy-start.26
  595.7 2.8 copy-start.27
  595.7 3.3 copy-start.12
  595.7 3.3 copy-start.14
  597.2 3.0 copy-start.6
  597.2 3.0 copy-start.28
  597.3 4.6 copy-start.20
  604.3 3.9 copy-start.8
  604.3 4.3 copy-start.10
  604.3 4.3 copy-start.25
  605.6 3.0 copy-start.23
  605.6 3.0 copy-start.24
  609.9 115.4 %reduce-scatter.19.cloned.1.call-start = ((), (), s32[]{:S(2)}) async-start(), calls=%async_computation.13 | async-start | bytes 1179648 | tf_op jit(solution)/shard_map/reduce_scatter | solution.py:260
  620.3 129.1 %reduce-scatter.39.cloned.1.call-start = ((), (), s32[]{:S(2)}) async-start(), calls=%async_computation.27 | async-start | bytes 811008
  633.1 176.1 %reduce-scatter.27.cloned.1.call-start = ((), (), s32[]{:S(2)}) async-start(), calls=%async_computation.17 | async-start | bytes 835584 | tf_op jit(solution)/shard_map/reduce_scatter | solution.py:330
  635.4 233.7 %reduce-scatter.29.cloned.1.call-start = ((), (), s32[]{:S(2)}) async-start(), calls=%async_computation.18 | async-start | bytes 835584 | tf_op jit(solution)/shard_map/reduce_scatter | solution.py:331
  637.7 310.3 %reduce-scatter.25.cloned.1.call-start = ((), (), s32[]{:S(2)}) async-start(), calls=%async_computation.16 | async-start | bytes 5013504 | tf_op jit(solution)/shard_map/reduce_scatter | solution.py:329
  640.7 1.1 copy-start.17
  640.7 1.2 copy-start.22
  640.8 386.5 %reduce-scatter.31.cloned.1.call-start = ((), (), s32[]{:S(2)}) async-start(), calls=%async_computation.19 | async-start | bytes 5013504 | tf_op jit(solution)/shard_map/reduce_scatter | solution.py:332
  644.9 650.8 %reduce-scatter.33.cloned.1.call-start = ((), (), s32[]{:S(2)}) async-start(), calls=%async_computation.20 | async-start | bytes 29245440 | tf_op jit(solution)/shard_map/reduce_scatter | solution.py:301
  658.9 905.3 %reduce-scatter.35.cloned.1.call-start = ((), (), s32[]{:S(2)}) async-start(), calls=%async_computation.21 | async-start | bytes 29245440 | tf_op jit(solution)/shard_map/reduce_scatter | solution.py:302
  671.9 1.1 copy-start.18
  671.9 1160.7 %reduce-scatter.37.cloned.1.call-start = ((), (), s32[]{:S(2)}) async-start(), calls=%async_computation.22 | async-start | bytes 29245440 | tf_op jit(solution)/shard_map/reduce_scatter | solution.py:303
  685.9 39.3 %copy-start.3 = (f32[128,1536]{1,0:T(8,128)S(1)}, f32[128,1536]{1,0:T(8,128)}, u32[]{:S(2)}) copy-start(f32[128,1536]{1,0:T(8,128)} %param.16) | copy-start | bytes 2359300
  685.9 39.3 %copy-start.15 = (bf16[128,1536]{1,0:T(8,128)(2,1)S(1)}, bf16[128,1536]{1,0:T(8,128)(2,1)}, u32[]{:S(2)}) copy-start(bf16[128,1536]{1,0:T(8,128)(2,1)} %reduce-scatter.21.cloned.1.call-done) | copy-start | bytes 1179652
  (5 other events, 4.1 us)
Sparse Core Ops, SparseCore 0:
  10.3 45.4 all-gather.15
  58.1 41.3 all-gather.17
  140.4 23.6 reduce-scatter.16
  166.3 129.8 all-gather.21
  298.4 138.9 all-gather.19
  562.3 13.3 reduce-scatter.20
  610.0 17.4 reduce-scatter.22
  630.4 17.4 reduce-scatter.18
  653.0 96.3 reduce-scatter.38
  753.4 55.7 reduce-scatter.26
  813.4 55.7 reduce-scatter.28
  873.4 74.5 reduce-scatter.24
  952.4 74.7 reduce-scatter.30
  1031.8 263.9 reduce-scatter.32
  1300.3 263.8 reduce-scatter.34
  1568.7 263.8 reduce-scatter.36
